TPU v7x, 32 devices: a whole 2x2x4 slice. The times are simulated.
32 devices in a mesh: row: 4 (over y, x), col: 4 (over z), depth: 2 (over core).
Axes of the slice: x: 2, y: 2, z: 4, core: 2. Of those that a mesh axis runs over, the one named last changes fastest.
Arguments:
- features: bfloat16 [4096, 768], P(('row', 'col', 'depth')), may hold values from -6 to 6
- w_value: bfloat16 [768, 3072], replicated, may hold values from -0.21875 to 0.21875
- att_src: bfloat16 [4, 768], replicated, may hold values from -12 to 12
- att_dst: bfloat16 [4, 768], replicated, may hold values from -0.3984375 to 0.3984375
- tile_cols: int32 [32, 8], P('row'), may hold values from 0 to 31, as said below
- tile_count: int32 [32], P('row'), may hold values from 2 to 8, as said below
- neighbours: int32 [4096, 16], P('row'), may hold values from 0 to 4095, as said below
Outputs:
- mixed: bfloat16 [4096, 768], P(('row', 'col', 'depth'))
Inputs may be any that keep to these rules, and one draw needn't show every extreme that they name: tile_cols[t, 0] is t itself and the 8 tiles of a row tile are distinct. Tile c lies in run c // 2 and in column group (c // 2) % 4. Of the 8 tiles of one row tile at most 2 lie in one column group, and some row tile lists 2 of one group among its first tile_count tiles. Every tile of row tile t lies in t's run or in one of the 7 runs that follow it, cyclically over 16 runs, and some listed tile lies in the last of these. `tile_count`: some row tile lists all 8. The 16 neighbours of node i are distinct, differ from i, and lie in tiles tile_cols[i // 128, s] with s < tile_count[i // 128].
All inputs are finite; a program needn't handle non-finite values.
Results may differ from a plain program's by a relative error of at most 0.0059.
Values may be sent and summed in bfloat16 or wider, within the bound.
No kernel may reach another device: no remote copies, remote signals or barrier semaphores. Data moves between devices by JAX's collectives and lax.ppermute only.
A program may use at most 64 MiB of HBM per device.

v0:
```python
import jax
import jax.numpy as jnp
from jax import lax
from jax.sharding import PartitionSpec as P

D = 768
HEADS = 4
TILE = 128
SLOTS = 8
KNN = 16
GMAX = 2
LEAK_SLOPE = 0.2
NEG_BIG = -1e30


def from_behind(array, axis, by):
    length = lax.axis_size(axis)
    return lax.ppermute(array, axis, [(i, (i + by) % length) for i in range(length)])


def leaky_relu(inputs):
    return jnp.where(inputs > 0, inputs, LEAK_SLOPE * inputs)


def head_matrix(attention):
    heads_total, head_width = attention.shape
    selector = (jnp.arange(heads_total)[:, None] == jnp.arange(heads_total)[None, :]).astype(
        attention.dtype
    )
    spread = attention[:, :, None] * selector[:, None, :]
    return spread.reshape(heads_total * head_width, heads_total)


def project_rows(shard_rows, w_value):
    return jnp.dot(shard_rows, w_value, preferred_element_type=jnp.float32).astype(jnp.bfloat16)


def on_device(features, w_value, att_src, att_dst, tile_cols, tile_count, neighbours):
    source_matrix = head_matrix(att_src)
    target_matrix = head_matrix(att_dst)
    row_devices = lax.axis_size("row")
    col_devices = lax.axis_size("col")
    depth_devices = lax.axis_size("depth")
    own_row = lax.axis_index("row")
    own_col = lax.axis_index("col")
    own_depth = lax.axis_index("depth")
    piece_rows = features.shape[0]
    per_device = piece_rows // TILE
    block_tiles = tile_cols.shape[0]
    projected = [project_rows(features, w_value)]
    for distance in (1, 2):
        arrived = from_behind(features, "row", -distance)
        projected.append(project_rows(arrived, w_value))
    values = jnp.concatenate(projected, axis=0)
    own_values = projected[0]
    own_source = jnp.dot(own_values, source_matrix, preferred_element_type=jnp.float32)
    column_target = jnp.dot(values, target_matrix, preferred_element_type=jnp.float32)
    block_source = lax.all_gather(own_source, ("col", "depth"), axis=0, tiled=True)
    slot_index = jnp.arange(SLOTS, dtype=jnp.int32)
    run_index = tile_cols // (per_device * depth_devices)
    group_index = run_index % col_devices
    row_home = run_index // col_devices
    depth_home = tile_cols // per_device % depth_devices
    inside = (
        (group_index == own_col)
        & (depth_home == own_depth)
        & (slot_index[None, :] < tile_count[:, None])
    )
    local_tile = (row_home - own_row) % row_devices * per_device + tile_cols % per_device
    ranking = jnp.cumsum(inside.astype(jnp.int32), axis=1) - 1
    choose = inside[:, None, :] & (
        ranking[:, None, :] == jnp.arange(GMAX, dtype=jnp.int32)[None, :, None]
    )
    present = jnp.any(choose, axis=2)
    chosen_tile = jnp.sum(jnp.where(choose, tile_cols[:, None, :], 0), axis=2)
    chosen_local = jnp.sum(jnp.where(choose, local_tile[:, None, :], 0), axis=2)
    row_tiles = own_row * block_tiles + jnp.arange(block_tiles, dtype=jnp.int32)
    value_tiles = values.reshape(-1, TILE, HEADS * D)
    target_tiles = column_target.reshape(-1, TILE, HEADS)
    source_tiles = block_source.reshape(block_tiles, TILE, HEADS)
    near_tiles = neighbours.reshape(block_tiles, TILE, KNN)
    column_pos = jnp.arange(TILE, dtype=jnp.int32)

    def tile_logits(source, near_ids, pick_tile, pick_local, pick_live, home_tile):
        target = jnp.transpose(target_tiles[pick_local], (2, 0, 1)).reshape(HEADS, 1, GMAX * TILE)
        logits = leaky_relu(jnp.transpose(source)[:, :, None] + target)
        near_tile = near_ids // TILE
        near_spot = near_ids % TILE
        tile_hit = near_tile[:, :, None] == pick_tile[None, None, :]
        spot_hit = near_spot[:, :, None] == column_pos[None, None, :]
        linked = jnp.any(tile_hit[:, :, :, None] & spot_hit[:, :, None, :], axis=1)
        itself = (pick_tile == home_tile)[None, :, None] & (
            column_pos[:, None, None] == column_pos[None, None, :]
        )
        linked = ((linked | itself) & pick_live[None, :, None]).reshape(TILE, GMAX * TILE)
        return (jnp.where(linked[None], logits, NEG_BIG), linked)

    tile_inputs = (source_tiles, near_tiles, chosen_tile, chosen_local, present, row_tiles)

    def local_stats(inputs):
        logits, linked = tile_logits(
            inputs[0], inputs[1], inputs[2], inputs[3], inputs[4], inputs[5]
        )
        row_max = jnp.max(logits, axis=2)
        weights = jnp.where(linked[None], jnp.exp(logits - row_max[:, :, None]), 0.0)
        return (row_max, jnp.sum(weights, axis=2))

    local_max, local_sum = lax.map(local_stats, tile_inputs)
    global_peak = lax.pmax(local_max.astype(jnp.bfloat16), ("col", "depth")).astype(local_max.dtype)
    global_total = lax.psum(local_sum * jnp.exp(local_max - global_peak), ("col", "depth"))

    def tile_mix(inputs):
        logits, linked = tile_logits(
            inputs[0], inputs[1], inputs[2], inputs[3], inputs[4], inputs[5]
        )
        tile_peak = inputs[6]
        tile_total = inputs[7]
        scaled = jnp.exp(logits - tile_peak[:, :, None]) / tile_total[:, :, None]
        weights = jnp.where(linked[None], scaled, 0.0).astype(jnp.bfloat16)
        gathered = value_tiles[inputs[3]].reshape(GMAX * TILE, HEADS, D)
        return jnp.einsum("hij,jhd->id", weights, gathered, preferred_element_type=jnp.float32)

    partial_sums = lax.map(tile_mix, tile_inputs + (global_peak, global_total)).reshape(
        block_tiles * TILE, D
    )
    mixed_rows = lax.psum_scatter(partial_sums, ("col", "depth"), scatter_dimension=0, tiled=True)
    return jax.nn.elu(mixed_rows / HEADS).astype(jnp.bfloat16)


def solution(mesh):
    placed = (
        P(("row", "col", "depth"), None),
        P(),
        P(),
        P(),
        P("row", None),
        P("row"),
        P("row", None),
    )
    return jax.shard_map(
        on_device,
        mesh=mesh,
        in_specs=placed,
        out_specs=P(("row", "col", "depth"), None),
        check_vma=False,
    )
```

profile of v0, /device:TPU:0, one launch (start us, length us, event | category | flops | bytes accessed | tf_op | source)
XLA Modules:
  0.0 234.0 jit_solution(7692492828668962442)
XLA Ops:
  6.5 3.1 %collective-permute-start.1 = (bf16[128,768]{1,0:T(8,128)(2,1)}, bf16[128,768]{1,0:T(8,128)(2,1)S(1)}, u32[]{:S(2)}, u32[]{:S(2)}) collective-permute-start(bf16[128,768]{1,0:T(8,128)(2,1)} %param.11), channel_id=1, source_target_pairs={{0,16},{8,24},{16,0},{24,8},{1,17},{9,25},{17,1},{25,9},{2,18},{10... | collective-permute-start | bytes 589832 | tf_op jit(solution)/shard_map/ppermute | solution.py:18
  9.6 1.4 collective-permute-start
  13.9 3.3 %convolution_convert_fusion.2 = bf16[128,3072]{1,0:T(8,128)(2,1)S(1)} fusion(bf16[128,768]{1,0:T(8,128)(2,1)} %param.11, bf16[768,3072]{1,0:T(8,128)(2,1)} %param.12), kind=kOutput, calls=%fused_computation.96 | convolution fusion | flops 604372992 | bytes 5701632 | tf_op jit(solution)/shard_map/dot_general | solution.py:35
  17.7 13.1 %all_gather.3 = f32[1024,4]{0,1:T(4,128)S(1)} all-gather(f32[128,4]{0,1:T(4,128)S(1)} %fusion.49), channel_id=1, replica_groups=mesh['row'=4,'col'=4,'depth'=2] {'col','depth'}, dimensions={0}, use_global_device_ids=true | all-gather | bytes 18432 | tf_op jit(solution)/shard_map/all_gather | solution.py:58
  30.8 3.1 %convolution_convert_fusion = bf16[128,3072]{1,0:T(8,128)(2,1)S(1)} fusion(bf16[128,768]{1,0:T(8,128)(2,1)S(1)} %collective-permute-done.1, bf16[768,3072]{1,0:T(8,128)(2,1)} %param.12), kind=kOutput, calls=%fused_computation.94 | convolution fusion | flops 604372992 | bytes 5701632 | tf_op jit(solution)/shard_map/dot_general | solution.py:35
  35.0 1.4 copy-done.1
  37.1 37.4 %while.30 = (s32[]{:T(128)}, f32[8,4,128]{2,1,0:T(4,128)S(1)}, f32[8,4,128]{2,1,0:T(4,128)S(1)}, s32[8,128,16]{1,2,0:T(8,128)S(1)}, s32[8,2]{1,0:T(8,128)S(1)}, ...) while((s32[]{:T(128)}, f32[8,4,128]{2,1,0:T(4,128)S(1)}, ...), condition=%wide.region_8.9_spmd.clone.clone, body=%wide.region_4.8_spmd.clone.clone.sunk | while | flops 3282954 | bytes 990427 | solution.py:108
  39.0 1.0 and_reduce_fusion.4
  43.7 1.0 and_reduce_fusion.4
  48.4 1.0 and_reduce_fusion.4
  53.0 1.0 and_reduce_fusion.4
  57.7 1.0 and_reduce_fusion.4
  62.4 1.0 and_reduce_fusion.4
  67.1 1.0 and_reduce_fusion.4
  71.7 1.0 and_reduce_fusion.4
  74.6 15.9 %pmax.7 = bf16[8,4,128]{2,1,0:T(4,128)(2,1)S(1)} all-reduce(bf16[8,4,128]{2,1,0:T(4,128)(2,1)S(1)} %convert_element_type.42), channel_id=1, replica_groups=mesh['row'=4,'col'=4,'depth'=2] {'col','depth'}, use_global_device_ids=true, to_apply=%region_9.10 | all-reduce | flops 4096 | bytes 16384 | tf_op jit(solution)/shard_map/pmax | solution.py:109
  90.5 25.9 %psum.7 = f32[8,4,128]{2,1,0:T(4,128)S(1)} all-reduce(f32[8,4,128]{2,1,0:T(4,128)S(1)} %bitcast.208), channel_id=1, replica_groups=mesh['row'=4,'col'=4,'depth'=2] {'col','depth'}, use_global_device_ids=true, to_apply=%region_10.11 | all-reduce | flops 4096 | bytes 32768 | tf_op jit(solution)/shard_map/psum | solution.py:110
  116.4 71.1 %while.31 = (s32[]{:T(128)}, f32[8,128,768]{2,1,0:T(8,128)}, s32[8,128,16]{1,2,0:T(8,128)S(1)}, s32[8,2]{1,0:T(8,128)S(1)}, s32[8]{0:T(128)S(1)}, /*index=5*/pre...) while((s32[]{:T(128)}, f32[8,128,768]{2,1,0:T(8,128)}, ...), condition=%wide.region_13.14_spmd.clone.clone, body=%wide.region_11.13_spmd.clone.clone.sunk | while | flops 203955216 | bytes 9207539 | solution.py:123
  119.8 2.3 gather_fusion.1
  122.1 1.2 reshape.497
  124.0 1.3 fusion.97
  127.1 1.0 and_reduce_fusion.5
  128.7 2.3 gather_fusion.1
  131.0 1.2 reshape.497
  132.8 1.3 fusion.97
  136.0 1.0 and_reduce_fusion.5
  137.5 2.3 gather_fusion.1
  139.9 1.2 reshape.497
  141.7 1.3 fusion.97
  146.4 2.3 gather_fusion.1
  148.7 1.2 reshape.497
  150.6 1.4 fusion.97
  155.3 2.3 gather_fusion.1
  157.6 1.2 reshape.497
  159.5 1.3 fusion.97
  162.7 1.0 and_reduce_fusion.5
  164.2 2.3 gather_fusion.1
  166.5 1.2 reshape.497
  168.3 1.4 fusion.97
  173.1 2.3 gather_fusion.1
  175.4 1.2 reshape.497
  177.3 1.3 fusion.97
  180.4 1.0 and_reduce_fusion.5
  182.0 2.3 gather_fusion.1
  184.3 1.2 reshape.497
  186.1 1.3 fusion.97
  187.5 37.8 %reduce-scatter.2.cloned.1.call-done = f32[128,768]{1,0:T(8,128)} async-done(((f32[1024,768]{1,0:T(8,128)}), f32[128,768]{1,0:T(8,128)}) %reduce-scatter.2.cloned.1.call-update) | async-done | bytes 393232 | tf_op jit(solution)/shard_map/reduce_scatter | solution.py:126
  225.3 1.8 fusion.48
  (370 shorter events, 61.1 us)
Async XLA Ops:
  6.5 24.3 %copy-start = (s32[1024,16]{0,1:T(8,128)S(1)}, s32[1024,16]{0,1:T(8,128)}, u32[]{:S(2)}) copy-start(s32[1024,16]{0,1:T(8,128)} %param.17) | copy-start | bytes 196612
  6.5 10.7 %copy-start.3 = (bf16[4,768]{1,0:T(4,128)(2,1)S(1)}, bf16[4,768]{1,0:T(4,128)(2,1)}, u32[]{:S(2)}) copy-start(bf16[4,768]{1,0:T(4,128)(2,1)} %param.14) | copy-start | bytes 18436
  6.5 10.8 %copy-start.4 = (bf16[4,768]{1,0:T(4,128)(2,1)S(1)}, bf16[4,768]{1,0:T(4,128)(2,1)}, u32[]{:S(2)}) copy-start(bf16[4,768]{1,0:T(4,128)(2,1)} %param.13) | copy-start | bytes 18436
  6.5 218.8 %reduce-scatter.2.cloned.1.call-start = ((), (), s32[]{:S(2)}) async-start(), calls=%async_computation.1 | async-start | bytes 3538944 | tf_op jit(solution)/shard_map/reduce_scatter | solution.py:126
  6.5 24.3 %collective-permute-start.1 = (bf16[128,768]{1,0:T(8,128)(2,1)}, bf16[128,768]{1,0:T(8,128)(2,1)S(1)}, u32[]{:S(2)}, u32[]{:S(2)}) collective-permute-start(bf16[128,768]{1,0:T(8,128)(2,1)} %param.11), channel_id=1, source_target_pairs={{0,16},{8,24},{16,0},{24,8},{1,17},{9,25},{17,1},{25,9},{2,18},{10... | collective-permute-start | bytes 589832 | tf_op jit(solution)/shard_map/ppermute | solution.py:18
  9.6 24.4 %collective-permute-start = (bf16[128,768]{1,0:T(8,128)(2,1)}, bf16[128,768]{1,0:T(8,128)(2,1)S(1)}, u32[]{:S(2)}, u32[]{:S(2)}) collective-permute-start(bf16[128,768]{1,0:T(8,128)(2,1)} %param.11), channel_id=1, source_target_pairs={{0,24},{8,0},{16,8},{24,16},{1,25},{9,1},{17,9},{25,17},{2,26},{10... | collective-permute-start | bytes 589832 | tf_op jit(solution)/shard_map/ppermute | solution.py:18
  17.4 16.6 %copy-start.2 = (bf16[768,3072]{1,0:T(8,128)(2,1)S(1)}, bf16[768,3072]{1,0:T(8,128)(2,1)}, u32[]{:S(2)}) copy-start(bf16[768,3072]{1,0:T(8,128)(2,1)} %param.12) | copy-start | bytes 14155780
  35.0 1.4 copy-start.1
Sparse Core Ops, SparseCore 0:
  187.6 37.6 reduce-scatter.1
where the time goes:
time: 235 us; the launch traced here: 234 us
  local copies, waits for them, and re-layouts  57.5 us (24%)
  blocking collectives  55 us (23%)
  other arithmetic  44.9 us (19%)
  waiting for transfers between devices  37.8 us (16%)
  matrix products  18.9 us (8%)
  between operations  13.6 us (6%)
  starting transfers between devices  4.5 us (2%)
    reduce_scatter x1, waiting for transfers between devices, on_device(): lax.psum_scatter(partial_sums, ('col', 'depth'), scatter_dimension=0, til...  37.8 us
    psum x1, blocking collectives, on_device(): lax.psum(local_sum * jnp.exp(local_max - global_peak), ('col', 'depth'))  25.9 us
    gather x8, local copies, waits for them, and re-layouts, tile_mix(): gathered = value_tiles[inputs[3]].reshape(GMAX * TILE, HEADS, D)  18.5 us
    pmax x1, blocking collectives, on_device(): lax.pmax(local_max.astype(jnp.bfloat16), ('col', 'depth'))  15.9 us
    reduce_or x16, other arithmetic, tile_logits(): linked = jnp.any(tile_hit[:, :, :, None] & spot_hit[:, :, None, :], axis=1)  15.5 us
    all_gather x1, blocking collectives, on_device(): lax.all_gather(own_source, ('col', 'depth'), axis=0, tiled=True)  13.1 us
    dot_general x8, matrix products, tile_mix(): jnp.einsum('hij,jhd->id', weights, gathered, preferred_element_type=jnp.f...  10.8 us
    reshape x8, local copies, waits for them, and re-layouts, tile_mix(): gathered = value_tiles[inputs[3]].reshape(GMAX * TILE, HEADS, D)  9.83 us
  transfers between devices with their start and end apart: 3, of which 1 were waited for; matrix products, arithmetic and copies ran while one was open for 4% of the time, Pallas kernels for 0%

commit v1 on v0

--- a/solution.py
+++ b/solution.py
@@ -107,7 +107,9 @@
 
     local_max, local_sum = lax.map(local_stats, tile_inputs)
     global_peak = lax.pmax(local_max.astype(jnp.bfloat16), ("col", "depth")).astype(local_max.dtype)
-    global_total = lax.psum(local_sum * jnp.exp(local_max - global_peak), ("col", "depth"))
+    global_total = jnp.sum(
+        lax.all_gather(local_sum * jnp.exp(local_max - global_peak), ("col", "depth")), axis=0
+    )
 
     def tile_mix(inputs):
         logits, linked = tile_logits(

time: 235 us -> 223 us (0.949)
  blocking collectives: 55 us -> 43 us
    psum x1 -> x0, blocking collectives: 25.9 us -> none  [on_device(): lax.psum(local_sum * jnp.exp(local_max - global_peak), ('col', 'depth'))]
    all_gather x0 -> x1, blocking collectives: none -> 14 us  [on_device(): lax.all_gather(local_sum * jnp.exp(local_max - global_peak), ('col', 'dep...]
where the time goes in v1:
time: 223 us; the launch traced here: 222 us
  local copies, waits for them, and re-layouts  57.5 us (26%)
  other arithmetic  45 us (20%)
  blocking collectives  43 us (19%)
  waiting for transfers between devices  37.9 us (17%)
  matrix products  19 us (9%)
  between operations  13.6 us (6%)
  starting transfers between devices  4.5 us (2%)
    reduce_scatter x1, waiting for transfers between devices, on_device(): lax.psum_scatter(partial_sums, ('col', 'depth'), scatter_dimension=0, til...  37.8 us
    gather x8, local copies, waits for them, and re-layouts, tile_mix(): gathered = value_tiles[inputs[3]].reshape(GMAX * TILE, HEADS, D)  18.5 us
    pmax x1, blocking collectives, on_device(): lax.pmax(local_max.astype(jnp.bfloat16), ('col', 'depth'))  15.9 us
    reduce_or x16, other arithmetic, tile_logits(): linked = jnp.any(tile_hit[:, :, :, None] & spot_hit[:, :, None, :], axis=1)  15.5 us
    all_gather x1, blocking collectives, on_device(): lax.all_gather(local_sum * jnp.exp(local_max - global_peak), ('col', 'dep...  14 us
    all_gather x1, blocking collectives, on_device(): lax.all_gather(own_source, ('col', 'depth'), axis=0, tiled=True)  13.1 us
    dot_general x8, matrix products, tile_mix(): jnp.einsum('hij,jhd->id', weights, gathered, preferred_element_type=jnp.f...  10.7 us
    reshape x8, local copies, waits for them, and re-layouts, tile_mix(): gathered = value_tiles[inputs[3]].reshape(GMAX * TILE, HEADS, D)  9.83 us
  transfers between devices with their start and end apart: 3, of which 1 were waited for; matrix products, arithmetic and copies ran while one was open for 4% of the time, Pallas kernels for 0%

profile of v1, /device:TPU:0, one launch (start us, length us, event | category | flops | bytes accessed | tf_op | source)
XLA Modules:
  0.0 222.2 jit_solution(16849581578967015308)
XLA Ops:
  6.5 3.1 %collective-permute-start.1 = (bf16[128,768]{1,0:T(8,128)(2,1)}, bf16[128,768]{1,0:T(8,128)(2,1)S(1)}, u32[]{:S(2)}, u32[]{:S(2)}) collective-permute-start(bf16[128,768]{1,0:T(8,128)(2,1)} %param.11), channel_id=1, source_target_pairs={{0,16},{8,24},{16,0},{24,8},{1,17},{9,25},{17,1},{25,9},{2,18},{10... | collective-permute-start | bytes 589832 | tf_op jit(solution)/shard_map/ppermute | solution.py:18
  9.6 1.4 collective-permute-start
  13.9 3.3 %convolution_convert_fusion.2 = bf16[128,3072]{1,0:T(8,128)(2,1)S(1)} fusion(bf16[128,768]{1,0:T(8,128)(2,1)} %param.11, bf16[768,3072]{1,0:T(8,128)(2,1)} %param.12), kind=kOutput, calls=%fused_computation.96 | convolution fusion | flops 604372992 | bytes 5701632 | tf_op jit(solution)/shard_map/dot_general | solution.py:35
  17.7 13.1 %all_gather.9 = f32[1024,4]{0,1:T(4,128)S(1)} all-gather(f32[128,4]{0,1:T(4,128)S(1)} %fusion.49), channel_id=1, replica_groups=mesh['row'=4,'col'=4,'depth'=2] {'col','depth'}, dimensions={0}, use_global_device_ids=true | all-gather | bytes 18432 | tf_op jit(solution)/shard_map/all_gather | solution.py:58
  30.8 3.2 %convolution_convert_fusion = bf16[128,3072]{1,0:T(8,128)(2,1)S(1)} fusion(bf16[128,768]{1,0:T(8,128)(2,1)S(1)} %collective-permute-done.1, bf16[768,3072]{1,0:T(8,128)(2,1)} %param.12), kind=kOutput, calls=%fused_computation.94 | convolution fusion | flops 604372992 | bytes 5701632 | tf_op jit(solution)/shard_map/dot_general | solution.py:35
  35.0 1.4 copy-done.1
  37.2 37.4 %while.30 = (s32[]{:T(128)}, f32[8,4,128]{2,1,0:T(4,128)S(1)}, f32[8,4,128]{2,1,0:T(4,128)S(1)}, s32[8,128,16]{1,2,0:T(8,128)S(1)}, s32[8,2]{1,0:T(8,128)S(1)}, ...) while((s32[]{:T(128)}, f32[8,4,128]{2,1,0:T(4,128)S(1)}, ...), condition=%wide.region_8.9_spmd.clone.clone, body=%wide.region_4.8_spmd.clone.clone.sunk | while | flops 3282954 | bytes 990427 | solution.py:108
  39.1 1.0 and_reduce_fusion.4
  43.7 1.0 and_reduce_fusion.4
  48.4 1.0 and_reduce_fusion.4
  53.1 1.0 and_reduce_fusion.4
  57.8 1.0 and_reduce_fusion.4
  62.4 1.0 and_reduce_fusion.4
  67.1 1.0 and_reduce_fusion.4
  71.8 1.0 and_reduce_fusion.4
  74.6 15.9 %pmax.7 = bf16[8,4,128]{2,1,0:T(4,128)(2,1)S(1)} all-reduce(bf16[8,4,128]{2,1,0:T(4,128)(2,1)S(1)} %convert_element_type.42), channel_id=1, replica_groups=mesh['row'=4,'col'=4,'depth'=2] {'col','depth'}, use_global_device_ids=true, to_apply=%region_9.10 | all-reduce | flops 4096 | bytes 16384 | tf_op jit(solution)/shard_map/pmax | solution.py:109
  90.6 14.0 %all-gather = f32[64,4,128]{2,1,0:T(4,128)S(1)} all-gather(f32[8,4,128]{2,1,0:T(4,128)S(1)} %bitcast.209), channel_id=2, replica_groups=mesh['row'=4,'col'=4,'depth'=2] {'col','depth'}, dimensions={0}, use_global_device_ids=true | all-gather | bytes 147456 | tf_op jit(solution)/shard_map/all_gather | solution.py:111
  104.6 71.1 %while.31 = (s32[]{:T(128)}, f32[8,128,768]{2,1,0:T(8,128)}, s32[8,128,16]{1,2,0:T(8,128)S(1)}, s32[8,2]{1,0:T(8,128)S(1)}, s32[8]{0:T(128)S(1)}, /*index=5*/pre...) while((s32[]{:T(128)}, f32[8,128,768]{2,1,0:T(8,128)}, ...), condition=%wide.region_13.14_spmd.clone.clone, body=%wide.region_11.13_spmd.clone.clone.sunk | while | flops 203955216 | bytes 9207539 | solution.py:125
  108.0 2.3 %gather_fusion.1 = bf16[2,128,3072]{2,1,0:T(8,128)(2,1)S(1)} fusion(bf16[3,128,3072]{2,1,0:T(8,128)(2,1)} %get-tuple-element.809, s32[1024]{0:T(1024)S(1)} %pad_clamp_fusion.5), kind=kCustom, calls=%fused_computation.2.clone.clone.1 | custom fusion | bytes 3145736 | tf_op jit(solution)/shard_map/while/body/eval_jaxpr/gather | solution.py:122
  110.3 1.2 reshape.498
  112.1 1.3 fusion.97
  116.8 2.3 %gather_fusion.1 = bf16[2,128,3072]{2,1,0:T(8,128)(2,1)S(1)} fusion(bf16[3,128,3072]{2,1,0:T(8,128)(2,1)} %get-tuple-element.809, s32[1024]{0:T(1024)S(1)} %pad_clamp_fusion.5), kind=kCustom, calls=%fused_computation.2.clone.clone.1 | custom fusion | bytes 3145736 | tf_op jit(solution)/shard_map/while/body/eval_jaxpr/gather | solution.py:122
  119.2 1.2 reshape.498
  121.0 1.3 fusion.97
  124.2 1.0 and_reduce_fusion.5
  125.7 2.3 %gather_fusion.1 = bf16[2,128,3072]{2,1,0:T(8,128)(2,1)S(1)} fusion(bf16[3,128,3072]{2,1,0:T(8,128)(2,1)} %get-tuple-element.809, s32[1024]{0:T(1024)S(1)} %pad_clamp_fusion.5), kind=kCustom, calls=%fused_computation.2.clone.clone.1 | custom fusion | bytes 3145736 | tf_op jit(solution)/shard_map/while/body/eval_jaxpr/gather | solution.py:122
  128.0 1.2 reshape.498
  129.9 1.3 fusion.97
  133.1 1.0 and_reduce_fusion.5
  134.6 2.3 %gather_fusion.1 = bf16[2,128,3072]{2,1,0:T(8,128)(2,1)S(1)} fusion(bf16[3,128,3072]{2,1,0:T(8,128)(2,1)} %get-tuple-element.809, s32[1024]{0:T(1024)S(1)} %pad_clamp_fusion.5), kind=kCustom, calls=%fused_computation.2.clone.clone.1 | custom fusion | bytes 3145736 | tf_op jit(solution)/shard_map/while/body/eval_jaxpr/gather | solution.py:122
  136.9 1.2 reshape.498
  138.7 1.4 fusion.97
  143.5 2.3 %gather_fusion.1 = bf16[2,128,3072]{2,1,0:T(8,128)(2,1)S(1)} fusion(bf16[3,128,3072]{2,1,0:T(8,128)(2,1)} %get-tuple-element.809, s32[1024]{0:T(1024)S(1)} %pad_clamp_fusion.5), kind=kCustom, calls=%fused_computation.2.clone.clone.1 | custom fusion | bytes 3145736 | tf_op jit(solution)/shard_map/while/body/eval_jaxpr/gather | solution.py:122
  145.8 1.2 reshape.498
  147.6 1.3 fusion.97
  150.8 1.0 and_reduce_fusion.5
  152.4 2.3 %gather_fusion.1 = bf16[2,128,3072]{2,1,0:T(8,128)(2,1)S(1)} fusion(bf16[3,128,3072]{2,1,0:T(8,128)(2,1)} %get-tuple-element.809, s32[1024]{0:T(1024)S(1)} %pad_clamp_fusion.5), kind=kCustom, calls=%fused_computation.2.clone.clone.1 | custom fusion | bytes 3145736 | tf_op jit(solution)/shard_map/while/body/eval_jaxpr/gather | solution.py:122
  154.7 1.2 reshape.498
  156.5 1.4 fusion.97
  159.7 1.0 and_reduce_fusion.5
  161.3 2.3 %gather_fusion.1 = bf16[2,128,3072]{2,1,0:T(8,128)(2,1)S(1)} fusion(bf16[3,128,3072]{2,1,0:T(8,128)(2,1)} %get-tuple-element.809, s32[1024]{0:T(1024)S(1)} %pad_clamp_fusion.5), kind=kCustom, calls=%fused_computation.2.clone.clone.1 | custom fusion | bytes 3145736 | tf_op jit(solution)/shard_map/while/body/eval_jaxpr/gather | solution.py:122
  163.6 1.2 reshape.498
  165.4 1.3 fusion.97
  170.1 2.3 %gather_fusion.1 = bf16[2,128,3072]{2,1,0:T(8,128)(2,1)S(1)} fusion(bf16[3,128,3072]{2,1,0:T(8,128)(2,1)} %get-tuple-element.809, s32[1024]{0:T(1024)S(1)} %pad_clamp_fusion.5), kind=kCustom, calls=%fused_computation.2.clone.clone.1 | custom fusion | bytes 3145736 | tf_op jit(solution)/shard_map/while/body/eval_jaxpr/gather | solution.py:122
  172.4 1.2 reshape.498
  174.3 1.3 fusion.97
  175.7 37.8 %reduce-scatter.2.cloned.1.call-done = f32[128,768]{1,0:T(8,128)} async-done(((f32[1024,768]{1,0:T(8,128)}), f32[128,768]{1,0:T(8,128)}) %reduce-scatter.2.cloned.1.call-update) | async-done | bytes 393232 | tf_op jit(solution)/shard_map/reduce_scatter | solution.py:128
  213.5 1.8 fusion.48
  (371 shorter events, 61.1 us)
Async XLA Ops:
  6.5 24.3 %copy-start = (s32[1024,16]{0,1:T(8,128)S(1)}, s32[1024,16]{0,1:T(8,128)}, u32[]{:S(2)}) copy-start(s32[1024,16]{0,1:T(8,128)} %param.17) | copy-start | bytes 196612
  6.5 10.7 %copy-start.3 = (bf16[4,768]{1,0:T(4,128)(2,1)S(1)}, bf16[4,768]{1,0:T(4,128)(2,1)}, u32[]{:S(2)}) copy-start(bf16[4,768]{1,0:T(4,128)(2,1)} %param.14) | copy-start | bytes 18436
  6.5 10.8 %copy-start.4 = (bf16[4,768]{1,0:T(4,128)(2,1)S(1)}, bf16[4,768]{1,0:T(4,128)(2,1)}, u32[]{:S(2)}) copy-start(bf16[4,768]{1,0:T(4,128)(2,1)} %param.13) | copy-start | bytes 18436
  6.5 206.9 %reduce-scatter.2.cloned.1.call-start = ((), (), s32[]{:S(2)}) async-start(), calls=%async_computation.1 | async-start | bytes 3538944 | tf_op jit(solution)/shard_map/reduce_scatter | solution.py:128
  6.5 24.3 %collective-permute-start.1 = (bf16[128,768]{1,0:T(8,128)(2,1)}, bf16[128,768]{1,0:T(8,128)(2,1)S(1)}, u32[]{:S(2)}, u32[]{:S(2)}) collective-permute-start(bf16[128,768]{1,0:T(8,128)(2,1)} %param.11), channel_id=1, source_target_pairs={{0,16},{8,24},{16,0},{24,8},{1,17},{9,25},{17,1},{25,9},{2,18},{10... | collective-permute-start | bytes 589832 | tf_op jit(solution)/shard_map/ppermute | solution.py:18
  9.6 24.4 %collective-permute-start = (bf16[128,768]{1,0:T(8,128)(2,1)}, bf16[128,768]{1,0:T(8,128)(2,1)S(1)}, u32[]{:S(2)}, u32[]{:S(2)}) collective-permute-start(bf16[128,768]{1,0:T(8,128)(2,1)} %param.11), channel_id=1, source_target_pairs={{0,24},{8,0},{16,8},{24,16},{1,25},{9,1},{17,9},{25,17},{2,26},{10... | collective-permute-start | bytes 589832 | tf_op jit(solution)/shard_map/ppermute | solution.py:18
  17.4 16.7 %copy-start.2 = (bf16[768,3072]{1,0:T(8,128)(2,1)S(1)}, bf16[768,3072]{1,0:T(8,128)(2,1)}, u32[]{:S(2)}) copy-start(bf16[768,3072]{1,0:T(8,128)(2,1)} %param.12) | copy-start | bytes 14155780
  35.0 1.4 copy-start.1
Sparse Core Ops, SparseCore 0:
  175.8 37.6 reduce-scatter.1
